TPU v7x, 32 devices: a whole 2x2x4 slice. The times are simulated.
32 devices in a mesh: layer: 2 (over y), latent: 8 (over z, x), tok: 2 (over core).
Axes of the slice: x: 2, y: 2, z: 4, core: 2. Of those that a mesh axis runs over, the one named last changes fastest.
Arguments:
- resid: bfloat16 [2, 384, 2304], P('layer', 'tok', 'latent'), may hold values from -6 to 6
- w_enc: bfloat16 [2, 2304, 2048], P('layer', None, 'latent'), may hold values from -0.09375 to 0.09375
- b_enc: float32 [2048], P('latent'), may hold values from -3 to 3
- w_dec: bfloat16 [2, 2048, 2304], P('layer', 'latent'), may hold values from -0.125 to 0.125
- b_dec: bfloat16 [2, 2304], P('layer', 'latent'), may hold values from -3 to 3
Outputs:
- grad_w_enc: bfloat16 [2, 2304, 2048], P('layer', 'tok', 'latent')
- grad_w_dec: bfloat16 [2, 2048, 2304], P('layer', 'latent')
All inputs are finite; a program needn't handle non-finite values.
Results may differ from a plain program's by a relative error of at most 0.023.
Values may be sent and summed in bfloat16 or wider, within the bound.
A program may use at most 64 MiB of HBM per device.

v0:
```python
import jax
import jax.numpy as jnp
from jax import lax
from jax.sharding import PartitionSpec as P

BETA = 4.0


def shards(resid, w_enc, b_enc, w_dec, b_dec):
    decoder = w_dec[0]
    x_full, bias_full = (
        lax.all_gather(resid, "latent", axis=2, tiled=True),
        lax.all_gather(b_dec.reshape(1, 1, -1), "latent", axis=2, tiled=True),
    )
    x_full = x_full[0]
    bias_full = bias_full.reshape(-1).astype(jnp.float32)
    tok_rows = x_full.shape[0]
    tokens = tok_rows * lax.axis_size("tok")
    partial_value = jnp.dot(x_full, w_enc[0], preferred_element_type=jnp.float32)
    pre = lax.psum(partial_value.astype(jnp.bfloat16), "layer").astype(jnp.float32) + b_enc
    act = (jax.nn.softplus(BETA * pre) / BETA).astype(jnp.bfloat16)
    slope = jax.nn.sigmoid(BETA * pre)
    recon = lax.psum(
        jnp.dot(act, decoder, preferred_element_type=jnp.float32).astype(jnp.bfloat16), "latent"
    ).astype(jnp.float32)
    grad_all = (2.0 / tokens * (recon + bias_full - x_full.astype(jnp.float32))).astype(
        jnp.bfloat16
    )
    dec_sum = lax.dot_general(
        act, grad_all, (((0,), (0,)), ((), ())), preferred_element_type=jnp.float32
    )
    rows_grad = lax.dot_general(
        grad_all, decoder, (((1,), (1,)), ((), ())), preferred_element_type=jnp.float32
    )
    act_grad = rows_grad
    dec_sum, act_grad = (dec_sum, act_grad)
    grad_act = lax.psum(act_grad.astype(jnp.bfloat16), "layer").astype(jnp.float32)
    grad_pre = (grad_act * slope).astype(jnp.bfloat16)
    grad_w_dec = lax.psum(dec_sum.astype(jnp.bfloat16), "tok")
    grad_w_enc = lax.psum_scatter(
        lax.dot_general(
            x_full, grad_pre, (((0,), (0,)), ((), ())), preferred_element_type=jnp.float32
        ).astype(jnp.bfloat16),
        "tok",
        scatter_dimension=0,
        tiled=True,
    )
    return (grad_w_enc[None], grad_w_dec[None])


def solution(mesh):
    placed = (
        P("layer", "tok", "latent"),
        P("layer", None, "latent"),
        P("latent"),
        P("layer", "latent", None),
        P("layer", "latent"),
    )
    return jax.shard_map(
        shards,
        mesh=mesh,
        in_specs=placed,
        out_specs=(P("layer", "tok", "latent"), P("layer", "latent", None)),
        check_vma=False,
    )
```

profile of v0, /device:TPU:0, one launch (start us, length us, event | category | flops | bytes accessed | tf_op | source)
XLA Modules:
  0.0 235.1 jit_solution(12181217095717214668)
XLA Ops:
  7.2 1.9 copy.8
  9.1 51.7 %all_gather.6 = bf16[1,192,2304]{1,0,2:T(2,128)(2,1)S(1)} all-gather(bf16[1,192,288]{1,0,2:T(2,128)(2,1)} %copy.8), channel_id=1, replica_groups=mesh['layer'=2,'latent'=8,'tok'=2] {'latent'}, dimensions={2}, use_global_device_ids=true | all-gather | bytes 995328 | tf_op jit(solution)/shard_map/all_gather | solution.py:12
  60.8 4.9 %copy.9 = bf16[1,192,2304]{2,1,0:T(8,128)(2,1)} copy(bf16[1,192,2304]{1,0,2:T(2,128)(2,1)S(1)} %all_gather.6) | data formatting | bytes 1769472 | tf_op jit(solution)/shard_map/all_gather | solution.py:12
  65.7 2.6 %fusion.7 = bf16[192,256]{1,0:T(8,128)(2,1)} fusion(bf16[1,2304,256]{2,1,0:T(8,128)(2,1)} %param.6, bf16[1,192,2304]{2,1,0:T(8,128)(2,1)} %copy.9), kind=kOutput, calls=%fused_computation.11 | convolution fusion | flops 226541568 | bytes 2162688 | tf_op jit(solution)/shard_map/dot_general | solution.py:19
  68.3 0.0 all-reduce.8.cloned.1.call-start
  68.4 20.0 %all-reduce.6.cloned.1.call-done = bf16[192,256]{1,0:T(8,128)(2,1)} async-done(((bf16[192,256]{1,0:T(8,128)(2,1)}), bf16[192,256]{1,0:T(8,128)(2,1)}) %all-reduce.6.cloned.1.call-update) | async-done | bytes 98320 | tf_op jit(solution)/shard_map/psum | solution.py:20
  88.3 2.3 convolution_convert_fusion.2
  90.7 0.0 all-reduce.10.cloned.1.call-start
  90.7 0.6 dynamic-slice
  92.0 0.3 dynamic-update-slice
  92.3 22.1 %all-reduce = bf16[2304]{0:T(1024)(128)(2,1)S(1)} all-reduce(bf16[2304]{0:T(1024)(128)(2,1)S(1)} %dynamic-update-slice), channel_id=2, replica_groups=mesh['layer'=2,'latent'=8,'tok'=2] {'latent'}, use_global_device_ids=true, to_apply=%add | all-reduce | flops 2304 | bytes 9216
  114.4 53.9 %all-reduce.8.cloned.1.call-done = bf16[192,2304]{1,0:T(8,128)(2,1)} async-done(((bf16[192,2304]{1,0:T(8,128)(2,1)}), bf16[192,2304]{1,0:T(8,128)(2,1)}) %all-reduce.8.cloned.1.call-update) | async-done | bytes 884752 | tf_op jit(solution)/shard_map/psum | solution.py:23
  168.3 2.4 %fusion.10 = bf16[192,256]{1,0:T(8,128)(2,1)} fusion(bf16[1,256,2304]{2,1,0:T(8,128)(2,1)S(1)} %copy-done, bf16[192,2304]{1,0:T(8,128)(2,1)} %all-reduce.8.cloned.1.call-done, bf16[1,192,2304]{2,1,0:T(8,128)(2,1)S(1)} %copy-done.1, f32[2304]{0:T(1024)S(1)} %convert_element_type.66), kind=kOutput, calls=%fused_computation.12 | convolution fusion | flops 229195776 | bytes 3056640 | tf_op jit(solution)/shard_map/dot_general | solution.py:32
  170.7 0.0 reduce-scatter.4.cloned.1.call-start
  170.8 20.7 %all-reduce.10.cloned.1.call-done = bf16[192,256]{1,0:T(8,128)(2,1)} async-done(((bf16[192,256]{1,0:T(8,128)(2,1)}), bf16[192,256]{1,0:T(8,128)(2,1)}) %all-reduce.10.cloned.1.call-update) | async-done | bytes 98320 | tf_op jit(solution)/shard_map/psum | solution.py:37
  191.4 1.4 fusion
  192.9 1.4 copy.11
  194.3 0.0 all-reduce.12.cloned.1.call-start
  194.4 2.9 %fusion.1 = bf16[1,256,2304]{2,1,0:T(8,128)(2,1)} fusion(bf16[192,2304]{1,0:T(8,128)(2,1)} %all-reduce.8.cloned.1.call-done, bf16[1,192,2304]{2,1,0:T(8,128)(2,1)S(1)} %copy-done.1, f32[2304]{0:T(1024)S(1)} %convert_element_type.66, bf16[192,256]{1,0:T(8,128)(2,1)S(1)} %copy-done.2, f32[256]{0:T(256)S(1)} %copy-done.4), kind=kOutput, calls=%fused_computation.4 | convolution fusion | flops 230277120 | bytes 3057664 | tf_op jit(solution)/shard_map/dot_general | solution.py:29
  197.3 5.7 %reduce-scatter.4.cloned.1.call-done = bf16[1152,256]{1,0:T(8,128)(2,1)} async-done(((bf16[2304,256]{1,0:T(8,128)(2,1)}), bf16[1152,256]{1,0:T(8,128)(2,1)}) %reduce-scatter.4.cloned.1.call-update) | async-done | bytes 589840
  203.0 1.4 copy.12
  204.4 1.1 copy.10
  205.4 20.7 %all-reduce.12.cloned.1.call-done = bf16[1,256,2304]{2,1,0:T(8,128)(2,1)} async-done(((bf16[1,256,2304]{2,1,0:T(8,128)(2,1)}), bf16[1,256,2304]{2,1,0:T(8,128)(2,1)}) %all-reduce.12.cloned.1.call-update) | async-done | bytes 1179664 | tf_op jit(solution)/shard_map/psum | solution.py:39
  226.2 2.4 %copy.18 = bf16[1,256,2304]{2,1,0:T(8,128)(2,1)} copy(bf16[1,256,2304]{2,1,0:T(8,128)(2,1)} %all-reduce.12.cloned.1.call-done) | data formatting | bytes 2359296
  (21 shorter events, 0.2 us)
Async XLA Ops:
  7.2 81.2 %copy-start = (bf16[1,256,2304]{2,1,0:T(8,128)(2,1)S(1)}, bf16[1,256,2304]{2,1,0:T(8,128)(2,1)}, u32[]{:S(2)}) copy-start(bf16[1,256,2304]{2,1,0:T(8,128)(2,1)} %param.8) | copy-start | bytes 3538948
  7.2 81.2 %all-reduce.6.cloned.1.call-start = ((), (), s32[]{:S(2)}) async-start(), calls=%async_computation.1 | async-start | bytes 196608 | tf_op jit(solution)/shard_map/psum | solution.py:20
  65.7 22.7 %copy-start.4 = (f32[256]{0:T(256)S(1)}, f32[256]{0:T(256)}, u32[]{:S(2)}) copy-start(f32[256]{0:T(256)} %param.7) | copy-start | bytes 3076
  68.3 22.5 %copy-start.5 = (u32[32]{0:T(128)S(1)}, u32[32]{0:T(128)}, u32[]{:S(2)}) copy-start(u32[32]{0:T(128)} %constant.17) | copy-start | bytes 388
  68.3 23.7 %copy-start.3 = (bf16[1,288]{1,0:T(2,128)(2,1)S(1)}, bf16[1,288]{1,0:T(2,128)(2,1)}, u32[]{:S(2)}) copy-start(bf16[1,288]{1,0:T(2,128)(2,1)} %param.9) | copy-start | bytes 1732
  68.3 100.0 %copy-start.1 = (bf16[1,192,2304]{2,1,0:T(8,128)(2,1)S(1)}, bf16[1,192,2304]{2,1,0:T(8,128)(2,1)}, u32[]{:S(2)}) copy-start(bf16[1,192,2304]{2,1,0:T(8,128)(2,1)} %copy.9) | copy-start | bytes 2654212
  68.3 100.0 %all-reduce.8.cloned.1.call-start = ((), (), s32[]{:S(2)}) async-start(), calls=%async_computation.2 | async-start | bytes 1769472 | tf_op jit(solution)/shard_map/psum | solution.py:23
  90.7 100.7 %all-reduce.10.cloned.1.call-start = ((), (), s32[]{:S(2)}) async-start(), calls=%async_computation.3 | async-start | bytes 196608 | tf_op jit(solution)/shard_map/psum | solution.py:37
  114.4 77.0 %copy-start.2 = (bf16[192,256]{1,0:T(8,128)(2,1)S(1)}, bf16[192,256]{1,0:T(8,128)(2,1)}, u32[]{:S(2)}) copy-start(bf16[192,256]{1,0:T(8,128)(2,1)} %all-reduce.6.cloned.1.call-done) | copy-start | bytes 294916
  170.7 32.3 %reduce-scatter.4.cloned.1.call-start = ((), (), s32[]{:S(2)}) async-start(), calls=%async_computation.5 | async-start | bytes 1769472
  194.3 31.8 %all-reduce.12.cloned.1.call-start = ((), (), s32[]{:S(2)}) async-start(), calls=%async_computation.4 | async-start | bytes 2359296 | tf_op jit(solution)/shard_map/psum | solution.py:39
Sparse Core Ops, SparseCore 0:
  68.4 19.8 all-reduce.5
  91.8 76.4 all-reduce.7
  171.1 20.2 all-reduce.9
  194.4 8.5 reduce-scatter.3
  205.2 20.9 all-reduce.11
where the time goes:
time: 235 us
  waiting for transfers between devices  121 us (51%)
  blocking collectives  73.7 us (31%)
  between operations  14.5 us (6%)
  local copies, waits for them, and re-layouts  13.9 us (6%)
  matrix products  11.6 us (5%)
    psum x1, waiting for transfers between devices, shards(): lax.psum(jnp.dot(act, decoder, preferred_element_type=jnp.float32).astype...  53.9 us
    all_gather x1, blocking collectives, shards(): lax.all_gather(resid, 'latent', axis=2, tiled=True)  51.7 us
    unnamed x1, blocking collectives  22.1 us
    psum x1, waiting for transfers between devices, shards(): grad_w_dec = lax.psum(dec_sum.astype(jnp.bfloat16), 'tok')  20.7 us
    psum x1, waiting for transfers between devices, shards(): lax.psum(act_grad.astype(jnp.bfloat16), 'layer').astype(jnp.float32)  20.7 us
    psum x1, waiting for transfers between devices, shards(): lax.psum(partial_value.astype(jnp.bfloat16), 'layer').astype(jnp.float32)  20 us
    unnamed x20, local copies, waits for them, and re-layouts  8.98 us
    unnamed x6, waiting for transfers between devices  5.8 us
  transfers between devices with their start and end apart: 5, of which 5 were waited for; matrix products, arithmetic and copies ran while one was open for 3% of the time, Pallas kernels for 0%

commit v1 on v0

--- a/solution.py
+++ b/solution.py
@@ -2,6 +2,7 @@
 import jax.numpy as jnp
 from jax import lax
 from jax.sharding import PartitionSpec as P
+from jax.lax import all_gather
 
 BETA = 4.0
 
@@ -20,8 +21,9 @@
     pre = lax.psum(partial_value.astype(jnp.bfloat16), "layer").astype(jnp.float32) + b_enc
     act = (jax.nn.softplus(BETA * pre) / BETA).astype(jnp.bfloat16)
     slope = jax.nn.sigmoid(BETA * pre)
-    recon = lax.psum(
-        jnp.dot(act, decoder, preferred_element_type=jnp.float32).astype(jnp.bfloat16), "latent"
+    prepare_seats_all_in = lambda u: all_gather(u, "latent").sum(axis=0)
+    recon = prepare_seats_all_in(
+        jnp.dot(act, decoder, preferred_element_type=jnp.float32).astype(jnp.bfloat16)
     ).astype(jnp.float32)
     grad_all = (2.0 / tokens * (recon + bias_full - x_full.astype(jnp.float32))).astype(
         jnp.bfloat16

time: 235 us -> 269 us (1.14)
  waiting for transfers between devices: 121 us -> 150 us
  other arithmetic: 0.03 us -> 4.53 us
    all_gather x0 -> x1, waiting for transfers between devices: none -> 84.5 us  [shards(): prepare_seats_all_in = lambda u: all_gather(u, 'latent').sum(axis=0)]
    psum x1 -> x0, waiting for transfers between devices: 53.9 us -> none  [shards(): lax.psum(jnp.dot(act, decoder, preferred_element_type=jnp.float32).astype...]
    reduce_sum x0 -> x1, other arithmetic: none -> 4.5 us  [shards(): prepare_seats_all_in = lambda u: all_gather(u, 'latent').sum(axis=0)]
    unnamed x20 -> x22, local copies, waits for them, and re-layouts: 8.98 us -> 8.99 us
  transfers between devices with their start and end apart: 5 -> 5, of which waited for: 5 -> 5; matrix products, arithmetic and copies ran while one was open for 3% -> 2% of each run, Pallas kernels for 0% -> 0%
where the time goes in v1:
time: 269 us; the launch traced here: 268 us
  waiting for transfers between devices  150 us (56%)
  blocking collectives  74.2 us (28%)
  between operations  14.5 us (5%)
  local copies, waits for them, and re-layouts  13.9 us (5%)
  matrix products  10.4 us (4%)
  other arithmetic  4.53 us (2%)
    all_gather x1, waiting for transfers between devices, shards(): prepare_seats_all_in = lambda u: all_gather(u, 'latent').sum(axis=0)  84.5 us
    all_gather x1, blocking collectives, shards(): lax.all_gather(resid, 'latent', axis=2, tiled=True)  51.7 us
    unnamed x1, blocking collectives  22.6 us
    psum x1, waiting for transfers between devices, shards(): grad_w_dec = lax.psum(dec_sum.astype(jnp.bfloat16), 'tok')  20.7 us
    psum x1, waiting for transfers between devices, shards(): lax.psum(partial_value.astype(jnp.bfloat16), 'layer').astype(jnp.float32)  20 us
    psum x1, waiting for transfers between devices, shards(): lax.psum(act_grad.astype(jnp.bfloat16), 'layer').astype(jnp.float32)  19.5 us
    unnamed x22, local copies, waits for them, and re-layouts  8.99 us
    unnamed x6, waiting for transfers between devices  5.8 us
  transfers between devices with their start and end apart: 5, of which 5 were waited for; matrix products, arithmetic and copies ran while one was open for 2% of the time, Pallas kernels for 0%

profile of v1, /device:TPU:0, one launch (start us, length us, event | category | flops | bytes accessed | tf_op | source)
XLA Modules:
  0.0 268.3 jit_solution(11278597014392750402)
XLA Ops:
  7.2 1.9 copy.10
  9.1 51.7 %all_gather.12 = bf16[1,192,2304]{1,0,2:T(2,128)(2,1)S(1)} all-gather(bf16[1,192,288]{1,0,2:T(2,128)(2,1)} %copy.10), channel_id=1, replica_groups=mesh['layer'=2,'latent'=8,'tok'=2] {'latent'}, dimensions={2}, use_global_device_ids=true | all-gather | bytes 995328 | tf_op jit(solution)/shard_map/all_gather | solution.py:13
  60.8 4.9 %copy.11 = bf16[1,192,2304]{2,1,0:T(8,128)(2,1)} copy(bf16[1,192,2304]{1,0,2:T(2,128)(2,1)S(1)} %all_gather.12) | data formatting | bytes 1769472 | tf_op jit(solution)/shard_map/all_gather | solution.py:13
  65.7 2.6 fusion.14
  68.3 0.0 all-gather.4.cloned.1.call-start
  68.4 20.0 %all-reduce.5.cloned.1.call-done = bf16[192,256]{1,0:T(8,128)(2,1)} async-done(((bf16[192,256]{1,0:T(8,128)(2,1)}), bf16[192,256]{1,0:T(8,128)(2,1)}) %all-reduce.5.cloned.1.call-update) | async-done | bytes 98320 | tf_op jit(solution)/shard_map/psum | solution.py:21
  88.3 2.3 convolution_convert_fusion.2
  90.7 0.0 all-reduce.7.cloned.1.call-start
  90.7 0.6 dynamic-slice
  92.0 0.3 dynamic-update-slice
  92.3 22.6 %all-reduce = bf16[2304]{0:T(1024)(128)(2,1)S(1)} all-reduce(bf16[2304]{0:T(1024)(128)(2,1)S(1)} %dynamic-update-slice), channel_id=3, replica_groups=mesh['layer'=2,'latent'=8,'tok'=2] {'latent'}, use_global_device_ids=true, to_apply=%add | all-reduce | flops 2304 | bytes 9216
  114.9 84.5 %all-gather.4.cloned.1.call-done = bf16[1536,2304]{1,0:T(8,128)(2,1)} async-done(((bf16[192,2304]{1,0:T(8,128)(2,1)}), bf16[1536,2304]{1,0:T(8,128)(2,1)}) %all-gather.4.cloned.1.call-update) | async-done | bytes 7077904 | tf_op jit(solution)/shard_map/all_gather | solution.py:24
  199.4 4.5 %reduce_sum.12 = bf16[192,2304]{1,0:T(8,128)(2,1)S(1)} reduce(bf16[8,192,2304]{2,1,0:T(8,128)(2,1)} %bitcast.45, bf16[]{:T(256)} %constant.11.clone.1), dimensions={0}, to_apply=%region_1.2 | reduce | flops 3096576 | bytes 7962626 | tf_op jit(solution)/shard_map/reduce_sum | solution.py:24
  203.9 1.2 fusion.17
  205.2 19.5 %all-reduce.7.cloned.1.call-done = bf16[192,256]{1,0:T(8,128)(2,1)} async-done(((bf16[192,256]{1,0:T(8,128)(2,1)}), bf16[192,256]{1,0:T(8,128)(2,1)}) %all-reduce.7.cloned.1.call-update) | async-done | bytes 98320 | tf_op jit(solution)/shard_map/psum | solution.py:39
  224.7 1.4 fusion
  226.1 1.4 copy.14
  227.5 0.0 all-reduce.9.cloned.1.call-start
  227.6 2.9 %fusion.1 = bf16[1,256,2304]{2,1,0:T(8,128)(2,1)} fusion(bf16[192,2304]{1,0:T(8,128)(2,1)} %copy-done.2, bf16[1,192,2304]{2,1,0:T(8,128)(2,1)S(1)} %copy-done.1, f32[2304]{0:T(1024)S(1)} %convert_element_type.94, bf16[192,256]{1,0:T(8,128)(2,1)S(1)} %copy-done.3, f32[256]{0:T(256)S(1)} %copy-done.5), kind=kOutput, calls=%fused_computation.4 | convolution fusion | flops 230277120 | bytes 3057664 | tf_op jit(solution)/shard_map/dot_general | solution.py:31
  230.5 5.7 %reduce-scatter.4.cloned.1.call-done = bf16[1152,256]{1,0:T(8,128)(2,1)} async-done(((bf16[2304,256]{1,0:T(8,128)(2,1)}), bf16[1152,256]{1,0:T(8,128)(2,1)}) %reduce-scatter.4.cloned.1.call-update) | async-done | bytes 589840
  236.2 1.4 copy.15
  237.6 1.1 copy.13
  238.6 20.7 %all-reduce.9.cloned.1.call-done = bf16[1,256,2304]{2,1,0:T(8,128)(2,1)} async-done(((bf16[1,256,2304]{2,1,0:T(8,128)(2,1)}), bf16[1,256,2304]{2,1,0:T(8,128)(2,1)}) %all-reduce.9.cloned.1.call-update) | async-done | bytes 1179664 | tf_op jit(solution)/shard_map/psum | solution.py:41
  259.4 2.4 copy.20
  (24 shorter events, 0.2 us)
Async XLA Ops:
  7.2 81.2 %copy-start = (bf16[1,256,2304]{2,1,0:T(8,128)(2,1)S(1)}, bf16[1,256,2304]{2,1,0:T(8,128)(2,1)}, u32[]{:S(2)}) copy-start(bf16[1,256,2304]{2,1,0:T(8,128)(2,1)} %param.8) | copy-start | bytes 3538948
  7.2 81.2 %all-reduce.5.cloned.1.call-start = ((), (), s32[]{:S(2)}) async-start(), calls=%async_computation.1 | async-start | bytes 196608 | tf_op jit(solution)/shard_map/psum | solution.py:21
  65.7 22.7 %copy-start.5 = (f32[256]{0:T(256)S(1)}, f32[256]{0:T(256)}, u32[]{:S(2)}) copy-start(f32[256]{0:T(256)} %param.7) | copy-start | bytes 3076
  68.3 22.5 %copy-start.6 = (u32[32]{0:T(128)S(1)}, u32[32]{0:T(128)}, u32[]{:S(2)}) copy-start(u32[32]{0:T(128)} %constant.20) | copy-start | bytes 388
  68.3 23.7 %copy-start.4 = (bf16[1,288]{1,0:T(2,128)(2,1)S(1)}, bf16[1,288]{1,0:T(2,128)(2,1)}, u32[]{:S(2)}) copy-start(bf16[1,288]{1,0:T(2,128)(2,1)} %param.9) | copy-start | bytes 1732
  68.3 131.1 %all-gather.4.cloned.1.call-start = ((), (), s32[]{:S(2)}) async-start(), calls=%async_computation.4 | async-start | bytes 7962624 | tf_op jit(solution)/shard_map/all_gather | solution.py:24
  90.7 134.0 %all-reduce.7.cloned.1.call-start = ((), (), s32[]{:S(2)}) async-start(), calls=%async_computation.2 | async-start | bytes 196608 | tf_op jit(solution)/shard_map/psum | solution.py:39
  199.4 4.5 %copy-start.1 = (bf16[1,192,2304]{2,1,0:T(8,128)(2,1)S(1)}, bf16[1,192,2304]{2,1,0:T(8,128)(2,1)}, u32[]{:S(2)}) copy-start(bf16[1,192,2304]{2,1,0:T(8,128)(2,1)} %copy.11) | copy-start | bytes 2654212
  203.9 1.2 copy-start.2
  203.9 20.8 %copy-start.3 = (bf16[192,256]{1,0:T(8,128)(2,1)S(1)}, bf16[192,256]{1,0:T(8,128)(2,1)}, u32[]{:S(2)}) copy-start(bf16[192,256]{1,0:T(8,128)(2,1)} %all-reduce.5.cloned.1.call-done) | copy-start | bytes 294916
  205.1 31.1 %reduce-scatter.4.cloned.1.call-start = ((), (), s32[]{:S(2)}) async-start(), calls=%async_computation.5 | async-start | bytes 1769472
  227.5 31.8 %all-reduce.9.cloned.1.call-start = ((), (), s32[]{:S(2)}) async-start(), calls=%async_computation.3 | async-start | bytes 2359296 | tf_op jit(solution)/shard_map/psum | solution.py:41
Sparse Core Ops, SparseCore 0:
  68.4 19.8 all-reduce.4
  90.8 108.5 all-gather.3
  205.2 19.3 all-reduce.6
  227.7 8.5 reduce-scatter.3
  238.4 20.9 all-reduce.8
